TPU v7x, 32 devices: a whole 2x2x4 slice. The times are simulated.
32 devices in a mesh: sec: 4 (over y, x), dom: 8 (over z, core).
Axes of the slice: x: 2, y: 2, z: 4, core: 2. Of those that a mesh axis runs over, the one named last changes fastest.
Arguments:
- state_init: float32 [4, 8, 6, 1536], P('sec', 'dom'), may hold values from -6 to 6
- right_side: float32 [4, 8, 6, 1536], P('sec', 'dom'), may hold values from -6 to 6
- diag_inverse: float32 [4, 8, 6, 6, 1536], P('sec', 'dom'), may hold values from -1.2 to 2, as said below
- face_block: bfloat16 [4, 8, 6, 6, 9216], P('sec', 'dom'), may hold values from -0.47851562 to 0.47851562
- face_target: int32 [4, 8, 9216], P('sec', 'dom'), may hold values from 0 to 1535
- face_source: int32 [4, 8, 9216], P('sec', 'dom'), may hold values from 0 to 3071, as said below
- face_count: int32 [4, 8], P('sec', 'dom'), may hold values from 4608 to 9216, as said below
- send_list: int32 [4, 8, 1536], P('sec', 'dom'), may hold values from 0 to 1535
- surf_cell: int32 [4, 8, 128], P('sec', 'dom'), may hold values from 0 to 1535
- surf_count: int32 [4, 8, 8], P('sec', 'dom'), may hold values from 0 to 16, as said below
- surf_map: float32 [4, 8, 3, 6, 128], P('sec', 'dom'), may hold values from -3 to 3
- surf_node: int32 [3, 8, 128], P(None, 'dom'), may hold values from 0 to 1535
Outputs:
- state_final: float32 [4, 8, 6, 1536], P('sec', 'dom')
Inputs may be any that keep to these rules, and one draw needn't show every extreme that they name: `face_source`: values below 1536 name the partition's own cells; a value 1536 + r * 192 + k names slot k of neighbour block r, which comes from partition d - offset r of the same section; only existing partitions are read, and each block is read in a leading run of its slots whose length differs from block to block; some block's run is 192 long. Only the first face_count entries of a partition's face lists are live; some partition lists 9216 live entries. Live slots of a flow partition towards structure partition o are its first surf_count slots of that block. Only some flow partitions (those at the wall, drawn from the seed) have live slots, each towards a few structure partitions of consecutive index (mod 8); some pair has 16 live slots. The structure section's row is zero and not read. `diag_inverse`: each block is a transposed block inverse; its diagonal entries are positive.
All inputs are finite; a program needn't handle non-finite values.
Results may differ from a plain program's by a relative error of at most 0.0003.
Values sent between devices are 32-bit elements; how exact they have to be, the bound alone decides.
A program may use at most 128 MiB of HBM per device.

v0:
```python
import jax
import jax.numpy as jnp
from jax import lax
from jax.sharding import PartitionSpec as P

NVAR = 6
NLOAD = 3
NBR = 8
ITERS = 2


neighbour_offsets = (1, -1, 2, -2, 3, -3, 4, -4)


def shifted(value, axis, steps):
    count = lax.axis_size(axis)
    first, last = (max(0, -steps), min(count, count - steps))
    return lax.ppermute(value, axis, [(source, source + steps) for source in range(first, last)])


def apply_blocks(blocks, vector):
    width = blocks.shape[-2]
    total = blocks[..., :, 0, :].astype(jnp.float32) * vector[..., 0:1, :]
    for column in range(1, width):
        total = (
            total
            + blocks[..., :, column, :].astype(jnp.float32) * vector[..., column : column + 1, :]
        )
    return total


def apply_transposed(blocks, vector):
    height = blocks.shape[-3]
    total = blocks[..., 0, :, :] * vector[..., 0:1, :]
    for row_index in range(1, height):
        total = total + blocks[..., row_index, :, :] * vector[..., row_index : row_index + 1, :]
    return total


def body(
    state_init,
    right_side,
    diag_inverse,
    face_block,
    face_target,
    face_source,
    face_count,
    send_list,
    surf_cell,
    surf_count,
    surf_map,
    surf_node,
):
    state = state_init[0, 0]
    source_terms = right_side[0, 0]
    inverse = diag_inverse[0, 0]
    blocks = face_block[0, 0]
    targets = face_target[0, 0]
    sources = face_source[0, 0]
    live_faces = face_count[0, 0]
    outgoing_cells = send_list[0, 0]
    surface_cells = surf_cell[0, 0]
    slot_counts = surf_count[0, 0]
    coupling_map = surf_map[0, 0]
    node_table = surf_node[:, 0]
    cells = state.shape[1]
    faces = blocks.shape[2]
    dom_size = lax.axis_size("dom")
    block_slots = outgoing_cells.shape[0] // NBR
    final_row = lax.axis_size("sec") - 1
    sec_index = lax.axis_index("sec")
    is_structure = sec_index == final_row
    capacity = surface_cells.shape[0] // dom_size
    face_mask = (jnp.arange(faces, dtype=jnp.int32) < live_faces).astype(jnp.float32)
    slot_mask = (
        (jnp.arange(capacity, dtype=jnp.int32)[None, :] < slot_counts[:, None])
        .reshape(-1)
        .astype(jnp.float32)
    )
    slot_mask = slot_mask * jnp.where(is_structure, 0.0, 1.0)
    own_row = jnp.minimum(sec_index, final_row - 1)
    own_nodes = lax.dynamic_index_in_dim(node_table, own_row, 0, keepdims=False)
    for sweep in range(ITERS):
        outgoing = state[:, outgoing_cells]
        pieces = []
        for index in range(NBR):
            block_out = outgoing[:, index * block_slots : (index + 1) * block_slots]
            pieces.append(shifted(block_out, "dom", neighbour_offsets[index]))
        ghosts = jnp.concatenate(pieces, axis=1)
        extended = jnp.concatenate([state, ghosts], axis=1)
        gathered = extended[:, sources]
        contrib = apply_blocks(blocks, gathered) * face_mask[None, :]
        face_terms = jnp.zeros((NVAR, cells), jnp.float32).at[:, targets].add(contrib)
        loads = apply_blocks(coupling_map, state[:, surface_cells]) * slot_mask[None, :]
        arrived = lax.all_to_all(loads, "dom", split_axis=1, concat_axis=1, tiled=True)
        displaced = jnp.where(is_structure, state[:NLOAD], 0.0)
        dense_loads = jnp.zeros((NLOAD, cells), jnp.float32).at[:, own_nodes].add(arrived)
        load_total, column_disp = lax.psum((dense_loads, displaced), "sec")
        looked_up = column_disp[:, own_nodes]
        returned = (
            lax.all_to_all(looked_up, "dom", split_axis=1, concat_axis=1, tiled=True)
            * slot_mask[None, :]
        )
        pushed = apply_transposed(coupling_map, returned)
        flow_coupling = jnp.zeros((NVAR, cells), jnp.float32).at[:, surface_cells].add(pushed)
        struct_coupling = jnp.concatenate(
            [load_total, jnp.zeros((NVAR - NLOAD, cells), jnp.float32)], axis=0
        )
        coupling = jnp.where(is_structure, struct_coupling, flow_coupling)
        state = apply_blocks(inverse, source_terms - face_terms - coupling)
    return state[None, None]


def solution(mesh):
    in_specs = (
        P("sec", "dom", None, None),
        P("sec", "dom", None, None),
        P("sec", "dom", None, None, None),
        P("sec", "dom", None, None, None),
        P("sec", "dom", None),
        P("sec", "dom", None),
        P("sec", "dom"),
        P("sec", "dom", None),
        P("sec", "dom", None),
        P("sec", "dom", None),
        P("sec", "dom", None, None, None),
        P(None, "dom", None),
    )
    out_specs = P("sec", "dom", None, None)
    return jax.shard_map(body, mesh=mesh, in_specs=in_specs, out_specs=out_specs, check_vma=False)
```

profile of v0, /device:TPU:0, one launch (start us, length us, event | category | flops | bytes accessed | tf_op | source)
XLA Modules:
  0.0 484.6 jit_solution(1774488598289809015)
XLA Ops:
  1.8 2.6 gather_fusion
  5.4 3.1 collective-permute-start
  9.8 6.9 %collective-permute-start.2 = (f32[6,192]{0,1:T(8,128)}, f32[6,192]{0,1:T(8,128)}, u32[]{:S(2)}, u32[]{:S(2)}) collective-permute-start(f32[6,192]{0,1:T(8,128)} %get-tuple-element.72), channel_id=1, source_target_pairs={{0,2},{1,3},{2,4},{3,5},{4,6},{5,7},{8,10},{9,11},{10,12},{11,13},... | collective-permute-start | bytes 13832 | tf_op jit(solution)/shard_map/ppermute | solution.py:18
  17.9 4.2 collective-permute-start.4
  24.9 4.0 all-to-all-start
  30.3 5.4 %fusion.54 = (bf16[6,1,9216]{2,1,0:T(2,128)(2,1)S(1)}, bf16[6,1,9216]{2,1,0:T(2,128)(2,1)S(1)}, bf16[6,1,9216]{2,1,0:T(2,128)(2,1)S(1)}, bf16[6,1,9216]{2,1,0:T(...) fusion(bf16[6,6,9216]{2,1,0:T(8,128)(2,1)} %bitcast.228), kind=kLoop, calls=%fused_computation.187 | loop fusion | flops 55296 | bytes 1437696 | tf_op jit(solution)/shard_map/slice | solution.py:27
  39.7 3.3 copy.137
  46.2 60.9 %all-reduce.3 = (f32[3,1536]{0,1:T(8,128)}, f32[3,1536]{0,1:T(8,128)}) all-reduce(f32[3,1536]{0,1:T(8,128)} %select_bitcast_fusion, f32[3,1536]{0,1:T(8,128)} %scatter_custom_fusion.1), channel_id=1, replica_groups=mesh['sec'=4,'dom'=8] {'sec'}, use_global_device_ids=true, to_apply=%region_3.4 | all-reduce | flops 9216 | bytes 73728 | tf_op jit(solution)/shard_map/psum | solution.py:98
  109.6 3.9 all-to-all-start.1
  115.7 5.4 %collective-permute-start.6 = (f32[6,192]{0,1:T(8,128)S(1)}, f32[6,192]{0,1:T(8,128)S(1)}, u32[]{:S(2)}, u32[]{:S(2)}) collective-permute-start(f32[6,192]{0,1:T(8,128)S(1)} %copy-done.24), channel_id=1, source_target_pairs={{0,4},{1,5},{2,6},{3,7},{8,12},{9,13},{10,14},{11,15},{16,20},{17,... | collective-permute-start | bytes 13832 | tf_op jit(solution)/shard_map/ppermute | solution.py:18
  126.3 5.9 %collective-permute-done.7 = f32[6,192]{0,1:T(8,128)S(1)} collective-permute-done((f32[6,192]{0,1:T(8,128)S(1)}, f32[6,192]{0,1:T(8,128)S(1)}, u32[]{:S(2)}, u32[]{:S(2)}) %collective-permute-start.7) | collective-permute-done | bytes 4640 | tf_op jit(solution)/shard_map/ppermute | solution.py:18
  132.3 31.0 %gather_fusion.1 = f32[9216,6]{1,0:T(8,128)} fusion(f32[6,3072]{0,1:T(8,128)S(1)} %constant_dynamic-update-slice_fusion, s32[9216]{0:T(1024)S(1)} %copy-done.8), kind=kCustom, calls=%fused_computation.1 | custom fusion | bytes 479232 | tf_op jit(solution)/shard_map/gather | solution.py:91
  163.2 23.4 %slice_reduce_fusion.11 = (f32[9216]{0:T(1024)S(1)}, f32[9216]{0:T(1024)S(1)}, f32[9216]{0:T(1024)S(1)}, f32[9216]{0:T(1024)S(1)}, f32[9216]{0:T(1024)S(1)}, /*index=5*/f32[9216]{0:T(1024)S(1)}) fusion(f32[6,9216]{0,1:T(8,128)} %bitcast.217), kind=kLoop, calls=%fused_computation.25 | loop fusion | bytes 442368 | tf_op jit(solution)/shard_map/slice | solution.py:23
  187.1 2.9 copy.145
  190.1 49.9 %scatter_custom_fusion = f32[6,1536]{0,1:T(8,128)S(1)} fusion(s32[9216]{0:T(1024)} %bitcast.235, f32[9216,6]{1,0:T(8,128)} %copy.145, f32[]{:T(128)} %constant.8.clone.1), kind=kCustom, calls=%fused_computation.76 | custom fusion | flops 55296 | bytes 37376 | tf_op jit(solution)/shard_map/scatter-add | solution.py:93
  244.8 2.3 slice_reduce_fusion.23
  247.1 2.6 constant_dynamic-update-slice_fusion.17
  249.8 4.9 %gather_fusion.4 = f32[1536,6]{1,0:T(8,128)} fusion(f32[6,1536]{0,1:T(8,128)} %get-tuple-element.52, s32[2048]{0:T(1024)S(1)} %pad_clamp_fusion), kind=kCustom, calls=%fused_computation.4 | custom fusion | bytes 79872 | tf_op jit(solution)/shard_map/gather | solution.py:84
  254.7 2.1 slice_select_fusion
  260.1 3.3 all-to-all-start.2
  265.5 2.9 collective-permute-start.8
  269.7 5.8 %collective-permute-start.10 = (f32[6,192]{0,1:T(8,128)}, f32[6,192]{0,1:T(8,128)}, u32[]{:S(2)}, u32[]{:S(2)}) collective-permute-start(f32[6,192]{0,1:T(8,128)} %get-tuple-element.64), channel_id=1, source_target_pairs={{0,2},{1,3},{2,4},{3,5},{4,6},{5,7},{8,10},{9,11},{10,12},{11,13},... | collective-permute-start | bytes 13832 | tf_op jit(solution)/shard_map/ppermute | solution.py:18
  276.8 4.1 collective-permute-start.12
  283.1 59.9 %all-reduce.2 = (f32[3,1536]{0,1:T(8,128)}, f32[3,1536]{0,1:T(8,128)}) all-reduce(f32[3,1536]{0,1:T(8,128)} %slice_select_fusion, f32[3,1536]{0,1:T(8,128)} %scatter_custom_fusion.4), channel_id=1, replica_groups=mesh['sec'=4,'dom'=8] {'sec'}, use_global_device_ids=true, to_apply=%region_8.9 | all-reduce | flops 9216 | bytes 73728 | tf_op jit(solution)/shard_map/psum | solution.py:98
  345.6 3.9 all-to-all-start.3
  351.7 5.4 %collective-permute-start.14 = (f32[6,192]{0,1:T(8,128)S(1)}, f32[6,192]{0,1:T(8,128)S(1)}, u32[]{:S(2)}, u32[]{:S(2)}) collective-permute-start(f32[6,192]{0,1:T(8,128)S(1)} %get-tuple-element.60), channel_id=1, source_target_pairs={{0,4},{1,5},{2,6},{3,7},{8,12},{9,13},{10,14},{11,15},{16,20},{17,... | collective-permute-start | bytes 13832 | tf_op jit(solution)/shard_map/ppermute | solution.py:18
  362.3 5.6 %collective-permute-done.15 = f32[6,192]{0,1:T(8,128)S(1)} collective-permute-done((f32[6,192]{0,1:T(8,128)S(1)}, f32[6,192]{0,1:T(8,128)S(1)}, u32[]{:S(2)}, u32[]{:S(2)}) %collective-permute-start.15) | collective-permute-done | bytes 4640 | tf_op jit(solution)/shard_map/ppermute | solution.py:18
  367.9 31.0 %gather_fusion.5 = f32[9216,6]{1,0:T(8,128)} fusion(f32[6,3072]{0,1:T(8,128)S(1)} %constant_dynamic-update-slice_fusion.9, s32[9216]{0:T(1024)S(1)} %copy-done.9), kind=kCustom, calls=%fused_computation.5 | custom fusion | bytes 479232 | tf_op jit(solution)/shard_map/gather | solution.py:91
  398.9 23.4 %slice_reduce_fusion.5 = (f32[9216]{0:T(1024)S(1)}, f32[9216]{0:T(1024)S(1)}, f32[9216]{0:T(1024)S(1)}, f32[9216]{0:T(1024)S(1)}, f32[9216]{0:T(1024)S(1)}, /*index=5*/f32[9216]{0:T(1024)S(1)}) fusion(f32[6,9216]{0,1:T(8,128)} %bitcast.216), kind=kLoop, calls=%fused_computation.19 | loop fusion | bytes 442368 | tf_op jit(solution)/shard_map/slice | solution.py:23
  422.8 2.9 copy.155
  425.7 49.9 %scatter_custom_fusion.3 = f32[6,1536]{0,1:T(8,128)S(1)} fusion(s32[9216]{0:T(1024)} %bitcast.236, f32[9216,6]{1,0:T(8,128)} %copy.155, f32[]{:T(128)} %constant.8.clone.1), kind=kCustom, calls=%fused_computation.72 | custom fusion | flops 55296 | bytes 37376 | tf_op jit(solution)/shard_map/scatter-add | solution.py:93
  479.7 2.3 slice_reduce_fusion.17
  (226 shorter events, 57.8 us)
Async XLA Ops:
  5.4 108.1 %collective-permute-start = (f32[6,192]{0,1:T(8,128)}, f32[6,192]{0,1:T(8,128)}, u32[]{:S(2)}, u32[]{:S(2)}) collective-permute-start(f32[6,192]{0,1:T(8,128)} %get-tuple-element.74), channel_id=1, source_target_pairs={{0,1},{1,2},{2,3},{3,4},{4,5},{5,6},{6,7},{8,9},{9,10},{10,11},{11... | collective-permute-start | bytes 13832 | tf_op jit(solution)/shard_map/ppermute | solution.py:18
  8.5 107.2 %collective-permute-start.1 = (f32[6,192]{0,1:T(8,128)}, f32[6,192]{0,1:T(8,128)}, u32[]{:S(2)}, u32[]{:S(2)}) collective-permute-start(f32[6,192]{0,1:T(8,128)} %get-tuple-element.73), channel_id=1, source_target_pairs={{1,0},{2,1},{3,2},{4,3},{5,4},{6,5},{7,6},{9,8},{10,9},{11,10},{12... | collective-permute-start | bytes 13832 | tf_op jit(solution)/shard_map/ppermute | solution.py:18
  9.8 112.3 %collective-permute-start.2 = (f32[6,192]{0,1:T(8,128)}, f32[6,192]{0,1:T(8,128)}, u32[]{:S(2)}, u32[]{:S(2)}) collective-permute-start(f32[6,192]{0,1:T(8,128)} %get-tuple-element.72), channel_id=1, source_target_pairs={{0,2},{1,3},{2,4},{3,5},{4,6},{5,7},{8,10},{9,11},{10,12},{11,13},... | collective-permute-start | bytes 13832 | tf_op jit(solution)/shard_map/ppermute | solution.py:18
  16.7 107.8 %collective-permute-start.3 = (f32[6,192]{0,1:T(8,128)}, f32[6,192]{0,1:T(8,128)}, u32[]{:S(2)}, u32[]{:S(2)}) collective-permute-start(f32[6,192]{0,1:T(8,128)} %get-tuple-element.71), channel_id=1, source_target_pairs={{2,0},{3,1},{4,2},{5,3},{6,4},{7,5},{10,8},{11,9},{12,10},{13,11},... | collective-permute-start | bytes 13832 | tf_op jit(solution)/shard_map/ppermute | solution.py:18
  17.9 107.4 %collective-permute-start.4 = (f32[6,192]{0,1:T(8,128)}, f32[6,192]{0,1:T(8,128)}, u32[]{:S(2)}, u32[]{:S(2)}) collective-permute-start(f32[6,192]{0,1:T(8,128)} %get-tuple-element.70), channel_id=1, source_target_pairs={{0,3},{1,4},{2,5},{3,6},{4,7},{8,11},{9,12},{10,13},{11,14},{12,15... | collective-permute-start | bytes 13832 | tf_op jit(solution)/shard_map/ppermute | solution.py:18
  24.9 18.5 %all-to-all-start = ((f32[3,8,16]{2,0,1:T(4,128)}), f32[3,8,16]{2,0,1:T(4,128)}, u32[]{:S(2)}, u32[]{:S(2)}) async-start(f32[3,8,16]{2,0,1:T(4,128)} %copy.146), calls=%async_computation | async-start | bytes 32768 | tf_op jit(solution)/shard_map/all_to_all | solution.py:95
  39.6 67.5 %copy-start.39 = (s32[1024]{0:T(1024)}, s32[1024]{0:T(1024)S(1)}, u32[]{:S(2)}) copy-start(s32[1024]{0:T(1024)S(1)} %pad_clamp_fusion.1) | copy-start | bytes 12292
  39.7 201.1 %copy-start.40 = (f32[128]{0:T(128)}, f32[128]{0:T(128)S(1)}, u32[]{:S(2)}) copy-start(f32[128]{0:T(128)S(1)} %mul.568) | copy-start | bytes 1540
  43.1 70.4 %copy-start.25 = (f32[6,192]{0,1:T(8,128)S(1)}, f32[6,192]{0,1:T(8,128)}, u32[]{:S(2)}) copy-start(f32[6,192]{0,1:T(8,128)} %get-tuple-element.69) | copy-start | bytes 13828
  43.4 72.4 %copy-start.24 = (f32[6,192]{0,1:T(8,128)S(1)}, f32[6,192]{0,1:T(8,128)}, u32[]{:S(2)}) copy-start(f32[6,192]{0,1:T(8,128)} %get-tuple-element.68) | copy-start | bytes 13828
  43.4 78.7 %copy-start.23 = (f32[6,192]{0,1:T(8,128)S(1)}, f32[6,192]{0,1:T(8,128)}, u32[]{:S(2)}) copy-start(f32[6,192]{0,1:T(8,128)} %get-tuple-element.67) | copy-start | bytes 13828
  46.2 86.0 %copy-start.8 = (s32[9216]{0:T(1024)S(1)}, s32[9216]{0:T(1024)}, u32[]{:S(2)}) copy-start(s32[9216]{0:T(1024)} %broadcast_clamp_fusion) | copy-start | bytes 110596
  109.6 130.4 %all-to-all-start.1 = ((f32[3,8,16]{2,0,1:T(4,128)}), f32[3,8,16]{2,0,1:T(4,128)}, u32[]{:S(2)}, u32[]{:S(2)}) async-start(f32[3,8,16]{2,0,1:T(4,128)} %copy.150), calls=%async_computation.1 | async-start | bytes 32768 | tf_op jit(solution)/shard_map/all_to_all | solution.py:101
  113.5 12.8 %collective-permute-start.5 = (f32[6,192]{0,1:T(8,128)S(1)}, f32[6,192]{0,1:T(8,128)S(1)}, u32[]{:S(2)}, u32[]{:S(2)}) collective-permute-start(f32[6,192]{0,1:T(8,128)S(1)} %copy-done.25), channel_id=1, source_target_pairs={{3,0},{4,1},{5,2},{6,3},{7,4},{11,8},{12,9},{13,10},{14,11},{15,12... | collective-permute-start | bytes 13832 | tf_op jit(solution)/shard_map/ppermute | solution.py:18
  115.7 10.6 %collective-permute-start.6 = (f32[6,192]{0,1:T(8,128)S(1)}, f32[6,192]{0,1:T(8,128)S(1)}, u32[]{:S(2)}, u32[]{:S(2)}) collective-permute-start(f32[6,192]{0,1:T(8,128)S(1)} %copy-done.24), channel_id=1, source_target_pairs={{0,4},{1,5},{2,6},{3,7},{8,12},{9,13},{10,14},{11,15},{16,20},{17,... | collective-permute-start | bytes 13832 | tf_op jit(solution)/shard_map/ppermute | solution.py:18
  122.1 10.2 %collective-permute-start.7 = (f32[6,192]{0,1:T(8,128)S(1)}, f32[6,192]{0,1:T(8,128)S(1)}, u32[]{:S(2)}, u32[]{:S(2)}) collective-permute-start(f32[6,192]{0,1:T(8,128)S(1)} %copy-done.23), channel_id=1, source_target_pairs={{4,0},{5,1},{6,2},{7,3},{12,8},{13,9},{14,10},{15,11},{20,16},{21,... | collective-permute-start | bytes 13832 | tf_op jit(solution)/shard_map/ppermute | solution.py:18
  187.1 53.7 %copy-start.32 = (f32[1,1,1,6,128]{4,1,3,2,0:T(1,128)S(1)}, f32[1,1,1,6,128]{4,1,3,2,0:T(1,128)}, u32[]{:S(2)}) copy-start(f32[1,1,1,6,128]{4,1,3,2,0:T(1,128)} %get-tuple-element.75) | copy-start | bytes 9220
  187.1 53.7 %copy-start.34 = (f32[1,1,1,6,128]{4,1,3,2,0:T(1,128)S(1)}, f32[1,1,1,6,128]{4,1,3,2,0:T(1,128)}, u32[]{:S(2)}) copy-start(f32[1,1,1,6,128]{4,1,3,2,0:T(1,128)} %get-tuple-element.76) | copy-start | bytes 9220
  260.1 20.8 %all-to-all-start.2 = ((f32[3,8,16]{2,0,1:T(4,128)}), f32[3,8,16]{2,0,1:T(4,128)S(1)}, u32[]{:S(2)}, u32[]{:S(2)}) async-start(f32[3,8,16]{2,0,1:T(4,128)} %copy.156), calls=%async_computation.2 | async-start | bytes 32768 | tf_op jit(solution)/shard_map/all_to_all | solution.py:95
  265.5 84.0 %collective-permute-start.8 = (f32[6,192]{0,1:T(8,128)}, f32[6,192]{0,1:T(8,128)}, u32[]{:S(2)}, u32[]{:S(2)}) collective-permute-start(f32[6,192]{0,1:T(8,128)} %get-tuple-element.66), channel_id=1, source_target_pairs={{0,1},{1,2},{2,3},{3,4},{4,5},{5,6},{6,7},{8,9},{9,10},{10,11},{11... | collective-permute-start | bytes 13832 | tf_op jit(solution)/shard_map/ppermute | solution.py:18
  268.4 83.3 %collective-permute-start.9 = (f32[6,192]{0,1:T(8,128)}, f32[6,192]{0,1:T(8,128)}, u32[]{:S(2)}, u32[]{:S(2)}) collective-permute-start(f32[6,192]{0,1:T(8,128)} %get-tuple-element.65), channel_id=1, source_target_pairs={{1,0},{2,1},{3,2},{4,3},{5,4},{6,5},{7,6},{9,8},{10,9},{11,10},{12... | collective-permute-start | bytes 13832 | tf_op jit(solution)/shard_map/ppermute | solution.py:18
  269.7 88.3 %collective-permute-start.10 = (f32[6,192]{0,1:T(8,128)}, f32[6,192]{0,1:T(8,128)}, u32[]{:S(2)}, u32[]{:S(2)}) collective-permute-start(f32[6,192]{0,1:T(8,128)} %get-tuple-element.64), channel_id=1, source_target_pairs={{0,2},{1,3},{2,4},{3,5},{4,6},{5,7},{8,10},{9,11},{10,12},{11,13},... | collective-permute-start | bytes 13832 | tf_op jit(solution)/shard_map/ppermute | solution.py:18
  275.5 85.0 %collective-permute-start.11 = (f32[6,192]{0,1:T(8,128)}, f32[6,192]{0,1:T(8,128)}, u32[]{:S(2)}, u32[]{:S(2)}) collective-permute-start(f32[6,192]{0,1:T(8,128)} %get-tuple-element.63), channel_id=1, source_target_pairs={{2,0},{3,1},{4,2},{5,3},{6,4},{7,5},{10,8},{11,9},{12,10},{13,11},... | collective-permute-start | bytes 13832 | tf_op jit(solution)/shard_map/ppermute | solution.py:18
  276.8 84.6 %collective-permute-start.12 = (f32[6,192]{0,1:T(8,128)S(1)}, f32[6,192]{0,1:T(8,128)}, u32[]{:S(2)}, u32[]{:S(2)}) collective-permute-start(f32[6,192]{0,1:T(8,128)S(1)} %get-tuple-element.62), channel_id=1, source_target_pairs={{0,3},{1,4},{2,5},{3,6},{4,7},{8,11},{9,12},{10,13},{11,14},{12,15... | collective-permute-start | bytes 13832 | tf_op jit(solution)/shard_map/ppermute | solution.py:18
  283.1 84.8 %copy-start.9 = (s32[9216]{0:T(1024)S(1)}, s32[9216]{0:T(1024)}, u32[]{:S(2)}) copy-start(s32[9216]{0:T(1024)} %broadcast_clamp_fusion) | copy-start | bytes 110596
  345.6 130.1 %all-to-all-start.3 = ((f32[3,8,16]{2,0,1:T(4,128)}), f32[3,8,16]{2,0,1:T(4,128)}, u32[]{:S(2)}, u32[]{:S(2)}) async-start(f32[3,8,16]{2,0,1:T(4,128)} %copy.159), calls=%async_computation.3 | async-start | bytes 32768 | tf_op jit(solution)/shard_map/all_to_all | solution.py:101
  349.5 12.8 %collective-permute-start.13 = (f32[6,192]{0,1:T(8,128)S(1)}, f32[6,192]{0,1:T(8,128)S(1)}, u32[]{:S(2)}, u32[]{:S(2)}) collective-permute-start(f32[6,192]{0,1:T(8,128)S(1)} %get-tuple-element.61), channel_id=1, source_target_pairs={{3,0},{4,1},{5,2},{6,3},{7,4},{11,8},{12,9},{13,10},{14,11},{15,12... | collective-permute-start | bytes 13832 | tf_op jit(solution)/shard_map/ppermute | solution.py:18
  351.7 10.6 %collective-permute-start.14 = (f32[6,192]{0,1:T(8,128)S(1)}, f32[6,192]{0,1:T(8,128)S(1)}, u32[]{:S(2)}, u32[]{:S(2)}) collective-permute-start(f32[6,192]{0,1:T(8,128)S(1)} %get-tuple-element.60), channel_id=1, source_target_pairs={{0,4},{1,5},{2,6},{3,7},{8,12},{9,13},{10,14},{11,15},{16,20},{17,... | collective-permute-start | bytes 13832 | tf_op jit(solution)/shard_map/ppermute | solution.py:18
  358.0 9.9 %collective-permute-start.15 = (f32[6,192]{0,1:T(8,128)S(1)}, f32[6,192]{0,1:T(8,128)S(1)}, u32[]{:S(2)}, u32[]{:S(2)}) collective-permute-start(f32[6,192]{0,1:T(8,128)S(1)} %get-tuple-element.59), channel_id=1, source_target_pairs={{4,0},{5,1},{6,2},{7,3},{12,8},{13,9},{14,10},{15,11},{20,16},{21,... | collective-permute-start | bytes 13832 | tf_op jit(solution)/shard_map/ppermute | solution.py:18
  422.8 53.7 %copy-start.33 = (f32[1,1,1,6,128]{4,1,3,2,0:T(1,128)S(1)}, f32[1,1,1,6,128]{4,1,3,2,0:T(1,128)}, u32[]{:S(2)}) copy-start(f32[1,1,1,6,128]{4,1,3,2,0:T(1,128)} %get-tuple-element.75) | copy-start | bytes 9220
  422.8 53.7 %copy-start.35 = (f32[1,1,1,6,128]{4,1,3,2,0:T(1,128)S(1)}, f32[1,1,1,6,128]{4,1,3,2,0:T(1,128)}, u32[]{:S(2)}) copy-start(f32[1,1,1,6,128]{4,1,3,2,0:T(1,128)} %get-tuple-element.76) | copy-start | bytes 9220
  422.8 53.7 %copy-start.37 = (f32[1,1,1,6,128]{4,1,3,2,0:T(1,128)S(1)}, f32[1,1,1,6,128]{4,1,3,2,0:T(1,128)}, u32[]{:S(2)}) copy-start(f32[1,1,1,6,128]{4,1,3,2,0:T(1,128)} %get-tuple-element.77) | copy-start | bytes 9220
  (39 other events, 574.6 us)
where the time goes:
time: 486 us; the launch traced here: 485 us
  local copies, waits for them, and re-layouts  160 us (33%)
  other arithmetic  127 us (26%)
  blocking collectives  121 us (25%)
  starting transfers between devices  63.6 us (13%)
  waiting for transfers between devices  11.5 us (2%)
    psum x2, blocking collectives, body(): load_total, column_disp = lax.psum((dense_loads, displaced), 'sec')  121 us
    scatter-add x2, other arithmetic, body(): jnp.zeros((NVAR, cells), jnp.float32).at[:, targets].add(contrib)  99.8 us
    gather x2, local copies, waits for them, and re-layouts, body(): gathered = extended[:, sources]  61.9 us
    slice x7, local copies, waits for them, and re-layouts, apply_blocks(): total = blocks[..., :, 0, :].astype(jnp.float32) * vector[..., 0:1, :]  52.2 us
    ppermute x16, starting transfers between devices, shifted(): lax.ppermute(value, axis, [(source, source + steps) for source in range(f...  48.6 us
    unnamed x119, local copies, waits for them, and re-layouts  14 us
    ppermute x16, waiting for transfers between devices, shifted(): lax.ppermute(value, axis, [(source, source + steps) for source in range(f...  11.5 us
  transfers between devices with their start and end apart: 20, of which 2 were waited for; matrix products, arithmetic and copies ran while one was open for 52% of the time, Pallas kernels for 0%

commit v1 on v0

v1 whole, which is shorter than its diff:
```python
import functools

import jax
import jax.numpy as jnp
from jax import lax
from jax.experimental import pallas as pl
from jax.experimental.pallas import tpu as pltpu
from jax.sharding import PartitionSpec as P

NVAR = 6
NLOAD = 3
NBR = 8
ITERS = 2
LANES = 128
ROWS = 8
LOW = 256
CHUNK = 512

neighbour_offsets = (1, -1, 2, -2, 3, -3, 4, -4)

F32 = jnp.float32
BF16 = jnp.bfloat16


def lane_gather(table, index):
    return jnp.take_along_axis(table, index, axis=1, mode="promise_in_bounds")


def spread(row):
    return jnp.broadcast_to(row, (ROWS, row.shape[-1]))


def gather_tiles(tiles, high, low):
    total = jnp.zeros((ROWS, LANES), F32)
    for at, tile in enumerate(tiles):
        total = jnp.where(high == at, lane_gather(tile, low), total)
    return total


def sum_rows(parts):
    width = parts[0].shape[1]
    row = lax.broadcasted_iota(jnp.int32, (ROWS, width), 0)
    parts = list(parts) + [None] * (ROWS - len(parts))
    step = ROWS // 2
    while step >= 1:
        upper = (row & step) == 0
        merged = []
        for at in range(step):
            a, b = parts[at], parts[at + step]
            if a is None and b is None:
                merged.append(None)
                continue
            if b is None:
                kept, moved = jnp.where(upper, a, 0.0), jnp.where(upper, 0.0, a)
            else:
                kept, moved = jnp.where(upper, a, b), jnp.where(upper, b, a)
            if step == ROWS // 2:
                moved = pltpu.roll(moved, step, 0)
            else:
                moved = jnp.where(upper, pltpu.roll(moved, ROWS - step, 0), pltpu.roll(moved, step, 0))
            merged.append(kept + moved)
        parts = merged
        step //= 2
    return parts[0]


def pad_rows(value):
    return jnp.concatenate([value, jnp.zeros((ROWS - value.shape[0], value.shape[1]), value.dtype)], axis=0)


def kernel(
    dims,
    state_init,
    right_side,
    inverse,
    face_block,
    face_target,
    face_source,
    face_count,
    send_list,
    surf_cell,
    surf_count,
    surf_map,
    surf_node,
    out_ref,
    state_buf,
    out_buf,
    halo_recv,
    ghost_buf,
    gath,
    onehot,
    load_send,
    load_recv,
    disp_send,
    disp_recv,
    halo_send_sem,
    halo_recv_sem,
    surf_send_sem,
    load_recv_sem,
    disp_recv_sem,
):
    n_sec, n_dom, cells, faces, slots, ghosts = dims
    flow = n_sec - 1
    tiles = cells // LANES
    ghost_tiles = ghosts // LANES
    block_slots = ghosts // NBR
    surf_tiles = slots // LANES
    cap = slots // n_dom
    per_tile = LANES // cap
    highs = cells // LOW
    sec = lax.axis_index("sec")
    dom = lax.axis_index("dom")
    is_structure = sec == flow
    lane = lax.broadcasted_iota(jnp.int32, (ROWS, LANES), 1)
    lane_block = lane // cap

    def present(offset):
        target = dom + offset
        return (target >= 0) & (target < n_dom)

    halo_recv[...] = jnp.zeros(halo_recv.shape, F32)
    load_recv[...] = jnp.zeros(load_recv.shape, F32)
    disp_recv[...] = jnp.zeros(disp_recv.shape, F32)

    barrier = pltpu.get_barrier_semaphore()
    for offset in neighbour_offsets:

        @pl.when(present(offset))
        def _():
            pl.semaphore_signal(barrier, inc=1, device_id={"dom": dom + offset})

    @pl.when(is_structure)
    def _():
        @pl.loop(0, flow * n_dom)
        def _(at):
            pl.semaphore_signal(barrier, inc=1, device_id={"sec": at // n_dom, "dom": at % n_dom})

    @pl.when(jnp.logical_not(is_structure))
    def _():
        @pl.loop(0, n_dom)
        def _(at):
            pl.semaphore_signal(barrier, inc=1, device_id={"sec": flow, "dom": at})

    expected = jnp.where(is_structure, flow * n_dom, n_dom)
    for offset in neighbour_offsets:
        expected = expected + present(offset).astype(jnp.int32)

    state_buf[...] = pad_rows(state_init[0, 0])
    live_faces = face_count[0, 0]

    def piece_tiles(index):
        start, end = index * block_slots, (index + 1) * block_slots
        return start, end, start // LANES, (end + LANES - 1) // LANES

    def halo_copy(sweep, index):
        _, _, first, last = piece_tiles(index)
        width = (last - first) * LANES
        return pltpu.make_async_remote_copy(
            src_ref=out_buf.at[sweep, :, pl.ds(first * LANES, width)],
            dst_ref=halo_recv.at[sweep, index, :, pl.ds(0, width)],
            send_sem=halo_send_sem.at[sweep, index],
            recv_sem=halo_recv_sem.at[sweep, index],
            device_id={"dom": dom + neighbour_offsets[index]},
        )

    def live_mask(tile):
        limit = jnp.zeros((ROWS, LANES), jnp.int32)
        for part in range(per_tile):
            limit = jnp.where(lane_block == part, surf_count[0, 0, tile * per_tile + part], limit)
        return (lane % cap) < limit

    def state_tiles():
        return [state_buf[:, at * LANES : (at + 1) * LANES] for at in range(tiles)]

    def prepare(sweep):
        own = state_tiles()
        for at in range(ghost_tiles):
            index = spread(send_list[0, :, at * LANES : (at + 1) * LANES])
            out_buf[sweep, :, at * LANES : (at + 1) * LANES] = gather_tiles(own, index // LANES, index % LANES)

    def prepare_surface(sweep):
        own = state_tiles()

        @pl.when(is_structure)
        def _():
            for section in range(flow):
                for tile in range(surf_tiles):
                    index = spread(surf_node[section, :, tile * LANES : (tile + 1) * LANES])
                    disp_send[sweep, section, tile] = gather_tiles(own, index // LANES, index % LANES)

        @pl.when(jnp.logical_not(is_structure))
        def _():
            for tile in range(surf_tiles):
                columns = slice(tile * LANES, (tile + 1) * LANES)
                index = spread(surf_cell[0, :, columns])
                values = gather_tiles(own, index // LANES, index % LANES)
                loads = sum_rows([pad_rows(surf_map[0, 0, row, :, columns] * values[:NVAR]) for row in range(NLOAD)])
                loads = jnp.where(live_mask(tile), loads, 0.0)
                mine = dom % per_tile
                for part in range(per_tile):
                    shift = lax.rem(mine - part + per_tile, per_tile) * cap
                    moved = pltpu.roll(loads, shift, 1)
                    load_send[sweep, tile * per_tile + part] = jnp.where(lane_block == mine, moved, 0.0)

    def send_halo(sweep):
        for index in range(NBR):

            @pl.when(present(neighbour_offsets[index]))
            def _():
                halo_copy(sweep, index).start()

    def send_surface(sweep):
        @pl.when(is_structure)
        def _():
            @pl.loop(0, flow * n_dom)
            def _(at):
                section, part = at // n_dom, at % n_dom
                pltpu.make_async_remote_copy(
                    src_ref=disp_send.at[sweep, section, part // per_tile],
                    dst_ref=disp_recv.at[sweep, dom],
                    send_sem=surf_send_sem.at[sweep],
                    recv_sem=disp_recv_sem.at[sweep],
                    device_id={"sec": section, "dom": part},
                ).start()

        @pl.when(jnp.logical_not(is_structure))
        def _():
            @pl.loop(0, n_dom)
            def _(at):
                pltpu.make_async_remote_copy(
                    src_ref=load_send.at[sweep, at],
                    dst_ref=load_recv.at[sweep, sec * n_dom + dom],
                    send_sem=surf_send_sem.at[sweep],
                    recv_sem=load_recv_sem.at[sweep],
                    device_id={"sec": flow, "dom": at},
                ).start()

    def build_onehot():
        step = CHUNK
        low_row = lax.broadcasted_iota(jnp.int32, (LOW, step), 0)

        @pl.loop(0, faces // step)
        def _(at):
            columns = pl.ds(pl.multiple_of(at * step, step), step)
            low = face_target[0, :, columns] % LOW
            onehot[:, columns] = jnp.where(low_row == low, 1.0, 0.0).astype(BF16)

    def local_gather():
        own = state_tiles()

        @pl.loop(0, faces // CHUNK)
        def _(at):
            for piece in range(CHUNK // LANES):
                columns = pl.ds(pl.multiple_of(at * CHUNK + piece * LANES, LANES), LANES)
                index = spread(face_source[0, :, columns])
                gath[:, columns] = gather_tiles(own, index // LANES, index % LANES)

    def receive_halo(sweep):
        for index in range(NBR):

            @pl.when(present(-neighbour_offsets[index]))
            def _():
                halo_copy(sweep, index).wait_recv()

        for at in range(ghost_tiles):
            total = jnp.zeros((ROWS, LANES), F32)
            for index in range(NBR):
                start, end, first, last = piece_tiles(index)
                if first <= at < last:
                    inside = (lane + at * LANES >= start) & (lane + at * LANES < end)
                    part = halo_recv[sweep, index, :, (at - first) * LANES : (at - first + 1) * LANES]
                    total = jnp.where(inside, part, total)
            ghost_buf[:, at * LANES : (at + 1) * LANES] = total

    def masked_dot(values, high, rhs):
        first = values.astype(BF16)
        second = (values - first.astype(F32)).astype(BF16)
        both = jnp.concatenate([first, second], axis=0)
        high = jnp.broadcast_to(high.astype(F32), both.shape).astype(BF16)
        lhs = jnp.concatenate(
            [jnp.where(high == at, both, jnp.zeros_like(both)) for at in range(highs)], axis=0
        )
        return lax.dot_general(lhs, rhs, (((1,), (1,)), ((), ())), preferred_element_type=F32)

    def face_pass():
        remote = [ghost_buf[:, at * LANES : (at + 1) * LANES] for at in range(ghost_tiles)]

        def step(at, total):
            base = at * CHUNK
            columns = pl.ds(pl.multiple_of(base, CHUNK), CHUNK)
            pieces = []
            for piece in range(CHUNK // LANES):
                part = pl.ds(pl.multiple_of(base + piece * LANES, LANES), LANES)
                index = spread(face_source[0, :, part])
                high, low = index // LANES, index % LANES
                value = gath[:, part]
                for tile in range(ghost_tiles):
                    value = jnp.where(high == tiles + tile, lane_gather(remote[tile], low), value)
                products = [
                    pad_rows(face_block[0, 0, row, :, part].astype(F32) * value[:NVAR]) for row in range(NVAR)
                ]
                pieces.append(sum_rows(products))
            contrib = jnp.concatenate(pieces, axis=1)
            entry = lax.broadcasted_iota(jnp.int32, (1, CHUNK), 1) + base
            high = jnp.where(entry < live_faces, face_target[0, :, columns] // LOW, highs)
            return total + masked_dot(contrib, high, onehot[:, columns])

        return lax.fori_loop(0, faces // CHUNK, step, jnp.zeros((2 * ROWS * highs, LOW), F32))

    def surface_pass(sweep):
        @pl.when(is_structure)
        def _():
            pltpu.make_async_copy(load_recv.at[sweep], load_recv.at[sweep], load_recv_sem.at[sweep]).wait()

        @pl.when(jnp.logical_not(is_structure))
        def _():
            pltpu.make_async_copy(disp_recv.at[sweep], disp_recv.at[sweep], disp_recv_sem.at[sweep]).wait()

        total = None
        low_row = lax.broadcasted_iota(jnp.int32, (LOW, LANES), 0)
        mine = dom % per_tile
        for section in range(flow):
            for tile in range(surf_tiles):
                columns = slice(tile * LANES, (tile + 1) * LANES)
                values = jnp.zeros((ROWS, LANES), F32)
                for part in range(per_tile):
                    values = values + load_recv[sweep, section * n_dom + tile * per_tile + part]
                cell = surf_node[section, :, columns]
                if section == 0:
                    back = jnp.zeros((ROWS, LANES), F32)
                    for part in range(per_tile):
                        shift = lax.rem(part - mine + per_tile, per_tile) * cap
                        moved = pltpu.roll(disp_recv[sweep, tile * per_tile + part], shift, 1)
                        back = jnp.where(lane_block == part, moved, back)
                    back = jnp.where(live_mask(tile), back, 0.0)
                    pushed = surf_map[0, 0, 0, :, columns] * back[0:1]
                    for row in range(1, NLOAD):
                        pushed = pushed + surf_map[0, 0, row, :, columns] * back[row : row + 1]
                    values = jnp.where(is_structure, values, pad_rows(pushed))
                    cell = jnp.where(is_structure, cell, surf_cell[0, :, columns])
                else:
                    values = jnp.where(is_structure, values, 0.0)
                rhs = jnp.where(low_row == cell % LOW, 1.0, 0.0).astype(BF16)
                term = masked_dot(values, cell // LOW, rhs)
                total = term if total is None else total + term
        return total

    prepare(0)
    prepare_surface(0)
    build_onehot()
    pl.semaphore_wait(barrier, expected)
    for sweep in range(ITERS):
        if sweep > 0:
            prepare(sweep)
            prepare_surface(sweep)
        send_halo(sweep)
        send_surface(sweep)
        local_gather()
        receive_halo(sweep)
        total = face_pass()
        total = total + surface_pass(sweep)
        for high in range(highs):
            base = 2 * ROWS * high
            columns = slice(high * LOW, (high + 1) * LOW)
            gone = total[base : base + ROWS] + total[base + ROWS : base + 2 * ROWS]
            rest = right_side[0, 0, :, columns] - gone[:NVAR]
            fresh = sum_rows([pad_rows(inverse[0, 0, row, :, columns] * rest) for row in range(NVAR)])
            if sweep == ITERS - 1:
                out_ref[0, 0, :, columns] = fresh[:NVAR]
            else:
                state_buf[:, columns] = fresh

    for sweep in range(ITERS):
        for index in range(NBR):

            @pl.when(present(neighbour_offsets[index]))
            def _():
                halo_copy(sweep, index).wait_send()

        @pl.when(is_structure)
        def _():
            pltpu.make_async_copy(load_recv.at[sweep], load_recv.at[sweep], surf_send_sem.at[sweep]).wait()

        @pl.when(jnp.logical_not(is_structure))
        def _():
            pltpu.make_async_copy(disp_recv.at[sweep], disp_recv.at[sweep], surf_send_sem.at[sweep]).wait()


def body(n_sec, n_dom, *args):
    cells = args[0].shape[-1]
    faces = args[4].shape[-1]
    ghosts = args[7].shape[-1]
    slots = args[8].shape[-1]
    flow = n_sec - 1
    piece = (2 * LANES - 1 + ghosts // NBR) // LANES * LANES
    vmem = pl.BlockSpec(memory_space=pltpu.VMEM)
    smem = pl.BlockSpec(memory_space=pltpu.SMEM)
    specs = [vmem] * 12
    specs[6] = smem
    specs[9] = smem
    return pl.pallas_call(
        functools.partial(kernel, (n_sec, n_dom, cells, faces, slots, ghosts)),
        out_shape=jax.ShapeDtypeStruct(args[0].shape, F32),
        in_specs=specs,
        out_specs=vmem,
        scratch_shapes=[
            pltpu.VMEM((ROWS, cells), F32),
            pltpu.VMEM((ITERS, ROWS, ghosts), F32),
            pltpu.VMEM((ITERS, NBR, ROWS, piece), F32),
            pltpu.VMEM((ROWS, ghosts), F32),
            pltpu.VMEM((ROWS, faces), F32),
            pltpu.VMEM((LOW, faces), BF16),
            pltpu.VMEM((ITERS, n_dom, ROWS, LANES), F32),
            pltpu.VMEM((ITERS, flow * n_dom, ROWS, LANES), F32),
            pltpu.VMEM((ITERS, flow, slots // LANES, ROWS, LANES), F32),
            pltpu.VMEM((ITERS, n_dom, ROWS, LANES), F32),
            pltpu.SemaphoreType.DMA((ITERS, NBR)),
            pltpu.SemaphoreType.DMA((ITERS, NBR)),
            pltpu.SemaphoreType.DMA((ITERS,)),
            pltpu.SemaphoreType.DMA((ITERS,)),
            pltpu.SemaphoreType.DMA((ITERS,)),
        ],
        compiler_params=pltpu.CompilerParams(
            collective_id=0, has_side_effects=True, vmem_limit_bytes=48 * 1024 * 1024
        ),
    )(*args)


def solution(mesh):
    in_specs = (
        P("sec", "dom", None, None),
        P("sec", "dom", None, None),
        P("sec", "dom", None, None, None),
        P("sec", "dom", None, None, None),
        P("sec", "dom", None),
        P("sec", "dom", None),
        P("sec", "dom"),
        P("sec", "dom", None),
        P("sec", "dom", None),
        P("sec", "dom", None),
        P("sec", "dom", None, None, None),
        P(None, "dom", None),
    )
    out_specs = P("sec", "dom", None, None)
    run = functools.partial(body, mesh.shape["sec"], mesh.shape["dom"])
    return jax.shard_map(run, mesh=mesh, in_specs=in_specs, out_specs=out_specs, check_vma=False)
```

time: 486 us -> 35.2 us (0.07)
  local copies, waits for them, and re-layouts: 160 us -> 4.36 us
  other arithmetic: 127 us -> 0 us
  blocking collectives: 121 us -> 0 us
  starting transfers between devices: 63.6 us -> 0 us
  Pallas kernels: 0 us -> 29.8 us
  waiting for transfers between devices: 11.5 us -> 0 us
    psum x2 -> x0, blocking collectives: 121 us -> none  [body(): load_total, column_disp = lax.psum((dense_loads, displaced), 'sec')]
    scatter-add x6 -> x0, other arithmetic: 107 us -> none  [the longest x2 99.8 us: body(): jnp.zeros((NVAR, cells), jnp.float32).at[:, targets].add(contrib)]
    gather x8 -> x0, local copies, waits for them, and re-layouts: 75.6 us -> none  [the longest x2 61.9 us: body(): gathered = extended[:, sources]]
    slice x13 -> x0, local copies, waits for them, and re-layouts: 56 us -> none  [the longest x7 52.2 us: apply_blocks(): total = blocks[..., :, 0, :].astype(jnp.float32) * vector[..., 0:1, :]]
    ppermute x16 -> x0, starting transfers between devices: 48.6 us -> none  [shifted(): lax.ppermute(value, axis, [(source, source + steps) for source in range(f...]
    pallas_call x0 -> x1, Pallas kernels: none -> 29.8 us  [body(): pl.pallas_call(functools.partial(kernel, (n_sec, n_dom, cells, faces, slo...]
    all_to_all x4 -> x0, starting transfers between devices: 15.1 us -> none  [the longest x2 7.75 us: body(): lax.all_to_all(looked_up, 'dom', split_axis=1, concat_axis=1, tiled=True)]
    ppermute x16 -> x0, waiting for transfers between devices: 11.5 us -> none  [shifted(): lax.ppermute(value, axis, [(source, source + steps) for source in range(f...]
  transfers between devices with their start and end apart: 20 -> 0, of which waited for: 2 -> 0; matrix products, arithmetic and copies ran while one was open for 52% -> 0% of each run, Pallas kernels for 0% -> 0%
where the time goes in v1:
time: 35.2 us; the launch traced here: 34.9 us
  Pallas kernels  29.8 us (85%)
  local copies, waits for them, and re-layouts  4.36 us (12%)
  between operations  0.78 us (2%)
    pallas_call x1, Pallas kernels, body(): pl.pallas_call(functools.partial(kernel, (n_sec, n_dom, cells, faces, slo...  29.8 us
    unnamed x20, local copies, waits for them, and re-layouts  3.7 us

profile of v1, /device:TPU:0, one launch (start us, length us, event | category | flops | bytes accessed | tf_op | source)
XLA Modules:
  0.0 34.9 jit_solution(568472650591712103)
XLA Ops:
  0.7 0.7 %copy.16.surf_map = f32[1,1,3,6,128]{4,3,2,1,0:T(8,128)S(1)} copy(f32[1,1,3,6,128]{4,1,3,2,0:T(1,128)} %param.22) | data formatting | bytes 18432 | tf_op args[10]
  1.4 0.0 copy-start.7
  1.4 0.8 %copy.13.state_init = f32[1,1,6,1536]{3,2,1,0:T(8,128)S(1)} copy(f32[1,1,6,1536]{3,1,2,0:T(1,128)} %param.12) | data formatting | bytes 73728 | tf_op args[0]
  2.1 0.0 copy-done.7
  2.2 0.0 copy-start.1
  2.2 0.0 copy-start.2
  2.2 0.0 copy-start.3
  2.2 0.0 copy-start.4
  2.2 0.0 copy-start.5
  2.2 0.0 copy-start.6
  2.2 1.0 %copy.15.inverse = f32[1,1,6,6,1536]{4,3,2,1,0:T(8,128)S(1)} copy(f32[1,1,6,6,1536]{4,1,3,2,0:T(1,128)} %param.14) | data formatting | bytes 442368 | tf_op args[2]
  3.2 0.0 copy-done.1
  3.3 0.0 copy-done.2
  3.3 0.0 copy-done.3
  3.3 0.0 copy-done.4
  3.3 0.0 copy-done.5
  3.3 0.0 copy-done.6
  3.3 0.0 copy-start
  3.3 1.2 %copy-done = bf16[1,1,6,6,9216]{4,3,2,1,0:T(8,128)(2,1)S(1)} copy-done((bf16[1,1,6,6,9216]{4,3,2,1,0:T(8,128)(2,1)S(1)}, bf16[1,1,6,6,9216]{4,3,2,1,0:T(8,128)(2,1)}, u32[]{:S(2)}) %copy-start) | copy-done | bytes 663576
  4.5 29.8 %shard_map.118 = f32[1,1,6,1536]{3,2,1,0:T(8,128)S(1)} custom-call(f32[1,1,6,1536]{3,2,1,0:T(8,128)S(1)} %copy.13.state_init, f32[1,1,6,1536]{3,2,1,0:T(8,128)S(1)} %copy.14.right_side, f32[1,1,6,6,1536]{4,3,2,1,0:T(8,128)S(1)} %copy.15.inverse, bf16[1,1,6,6,9216]{4,3,2,1,0:T(8,128)(2,1)S(1)} %copy-done, s32[1,1,9216]{2,1,0:T(1,128)S(1)} %copy-done.1, ...), custom_call_target="tpu_custom_call" | custom-call | tf_op jit(solution)/shard_map/pallas_call | solution.py:401
  34.3 0.7 %copy.17 = f32[1,1,6,1536]{3,1,2,0:T(1,128)} copy(f32[1,1,6,1536]{3,2,1,0:T(8,128)S(1)} %shard_map.118) | data formatting | bytes 73728 | tf_op jit(solution)/shard_map/pallas_call | solution.py:401
  (1 shorter events, 0.0 us)
Async XLA Ops:
  1.4 0.8 %copy-start.7 = (f32[1,1,6,1536]{3,1,2,0:T(1,128)S(1)}, f32[1,1,6,1536]{3,1,2,0:T(1,128)}, u32[]{:S(2)}) copy-start(f32[1,1,6,1536]{3,1,2,0:T(1,128)} %param.13) | copy-start | bytes 110596
  2.2 1.1 %copy-start.1 = (s32[1,1,9216]{2,1,0:T(1,128)S(1)}, s32[1,1,9216]{2,1,0:T(1,128)}, u32[]{:S(2)}) copy-start(s32[1,1,9216]{2,1,0:T(1,128)} %face_target.1) | copy-start | bytes 110596
  2.2 1.1 %copy-start.2 = (s32[1,1,9216]{2,1,0:T(1,128)S(1)}, s32[1,1,9216]{2,1,0:T(1,128)}, u32[]{:S(2)}) copy-start(s32[1,1,9216]{2,1,0:T(1,128)} %face_source.1) | copy-start | bytes 110596
  2.2 1.1 %copy-start.3 = (s32[1,1,1536]{2,1,0:T(1,128)S(1)}, s32[1,1,1536]{2,1,0:T(1,128)}, u32[]{:S(2)}) copy-start(s32[1,1,1536]{2,1,0:T(1,128)} %send_list.1) | copy-start | bytes 18436
  2.2 1.1 %copy-start.4 = (s32[3,1,128]{2,1,0:T(1,128)S(1)}, s32[3,1,128]{2,1,0:T(1,128)}, u32[]{:S(2)}) copy-start(s32[3,1,128]{2,1,0:T(1,128)} %surf_node.1) | copy-start | bytes 4612
  2.2 1.1 %copy-start.5 = (s32[1,1,128]{2,1,0:T(1,128)S(1)}, s32[1,1,128]{2,1,0:T(1,128)}, u32[]{:S(2)}) copy-start(s32[1,1,128]{2,1,0:T(1,128)} %surf_cell.1) | copy-start | bytes 1540
  2.2 1.1 %copy-start.6 = (s32[1,1,8]{2,1,0:T(1,128)S(1)}, s32[1,1,8]{2,1,0:T(1,128)}, u32[]{:S(2)}) copy-start(s32[1,1,8]{2,1,0:T(1,128)} %surf_count.1) | copy-start | bytes 100
  3.3 1.2 %copy-start = (bf16[1,1,6,6,9216]{4,3,2,1,0:T(8,128)(2,1)S(1)}, bf16[1,1,6,6,9216]{4,3,2,1,0:T(8,128)(2,1)}, u32[]{:S(2)}) copy-start(bf16[1,1,6,6,9216]{4,3,2,1,0:T(8,128)(2,1)} %face_block.1) | copy-start | bytes 1990660

commit v2 on v1

v2 whole, which is shorter than its diff:
```python
import functools

import jax
import jax.numpy as jnp
from jax import lax
from jax.experimental import pallas as pl
from jax.experimental.pallas import tpu as pltpu
from jax.sharding import PartitionSpec as P

NVAR = 6
NLOAD = 3
NBR = 8
ITERS = 2
LANES = 128
ROWS = 8
LOW = 256
WIDE = 256
CHUNK = 3072

neighbour_offsets = (1, -1, 2, -2, 3, -3, 4, -4)

F32 = jnp.float32
BF16 = jnp.bfloat16


def lane_gather(table, index):
    return jnp.take_along_axis(table, index, axis=1, mode="promise_in_bounds")


def spread(row):
    return jnp.broadcast_to(row, (ROWS, row.shape[-1]))


def gather_tiles(tiles, high, low):
    total = jnp.zeros((ROWS, LANES), F32)
    for at, tile in enumerate(tiles):
        total = jnp.where(high == at, lane_gather(tile, low), total)
    return total


def sum_rows(parts):
    width = parts[0].shape[1]
    row = lax.broadcasted_iota(jnp.int32, (ROWS, width), 0)
    parts = list(parts) + [None] * (ROWS - len(parts))
    step = ROWS // 2
    while step >= 1:
        upper = (row & step) == 0
        merged = []
        for at in range(step):
            a, b = parts[at], parts[at + step]
            if a is None and b is None:
                merged.append(None)
                continue
            if b is None:
                kept, moved = jnp.where(upper, a, 0.0), jnp.where(upper, 0.0, a)
            else:
                kept, moved = jnp.where(upper, a, b), jnp.where(upper, b, a)
            if step == ROWS // 2:
                moved = pltpu.roll(moved, step, 0)
            else:
                moved = jnp.where(upper, pltpu.roll(moved, ROWS - step, 0), pltpu.roll(moved, step, 0))
            merged.append(kept + moved)
        parts = merged
        step //= 2
    return parts[0]


def pad_rows(value):
    return jnp.concatenate([value, jnp.zeros((ROWS - value.shape[0], value.shape[1]), value.dtype)], axis=0)


def kernel(
    dims,
    state_init,
    right_side,
    inverse,
    face_block,
    face_target,
    face_source,
    face_count,
    send_list,
    surf_cell,
    surf_count,
    surf_map,
    surf_node,
    out_ref,
    init_v,
    right_v,
    inverse_v,
    block_v,
    target_v,
    source_v,
    list_v,
    cell_v,
    map_v,
    node_v,
    state_buf,
    state_lhs,
    ghost_lhs,
    out_hot,
    source_hot,
    out_buf,
    halo_recv,
    ghost_buf,
    gath,
    onehot,
    load_send,
    load_recv,
    disp_send,
    disp_recv,
    halo_send_sem,
    halo_recv_sem,
    surf_send_sem,
    load_recv_sem,
    disp_recv_sem,
    fetch_sem,
    ready_sem,
):
    n_sec, n_dom, cells, faces, slots, ghosts = dims
    flow = n_sec - 1
    tiles = cells // LANES
    ghost_tiles = ghosts // LANES
    block_slots = ghosts // NBR
    surf_tiles = slots // LANES
    cap = slots // n_dom
    per_tile = LANES // cap
    highs = cells // LOW
    sec = lax.axis_index("sec")
    dom = lax.axis_index("dom")
    is_structure = sec == flow
    lane = lax.broadcasted_iota(jnp.int32, (ROWS, LANES), 1)
    lane_block = lane // cap

    def present(offset):
        target = dom + offset
        return (target >= 0) & (target < n_dom)

    order = (
        (state_init, init_v),
        (send_list, list_v),
        (surf_node, node_v),
        (surf_cell, cell_v),
        (surf_map, map_v),
        (face_source, source_v),
        (face_target, target_v),
        (face_block, block_v),
        (right_side, right_v),
        (inverse, inverse_v),
    )
    fetches = [pltpu.make_async_copy(src, dst, fetch_sem.at[at]) for at, (src, dst) in enumerate(order)]
    for fetch in fetches:
        fetch.start()

    halo_recv[...] = jnp.zeros(halo_recv.shape, F32)
    load_recv[...] = jnp.zeros(load_recv.shape, F32)
    disp_recv[...] = jnp.zeros(disp_recv.shape, F32)

    barrier = pltpu.get_barrier_semaphore()

    @pl.loop(0, n_dom)
    def _(at):
        @pl.when(at != dom)
        def _():
            pl.semaphore_signal(barrier, inc=1, device_id={"dom": at})

    def greet(sem):
        @pl.when(is_structure)
        def _():
            for section in range(flow):
                pl.semaphore_signal(sem, inc=1, device_id={"sec": section})

        @pl.when(jnp.logical_not(is_structure))
        def _():
            pl.semaphore_signal(sem, inc=1, device_id={"sec": flow})

    greet(barrier)
    partners = jnp.where(is_structure, flow, 1)

    live_faces = face_count[0, 0]

    def piece_tiles(index):
        start, end = index * block_slots, (index + 1) * block_slots
        return start, end, start // LANES, (end + LANES - 1) // LANES

    def halo_copy(sweep, index):
        _, _, first, last = piece_tiles(index)
        width = (last - first) * LANES
        return pltpu.make_async_remote_copy(
            src_ref=out_buf.at[sweep, :, pl.ds(first * LANES, width)],
            dst_ref=halo_recv.at[sweep, index, :, pl.ds(0, width)],
            send_sem=halo_send_sem.at[sweep, index],
            recv_sem=halo_recv_sem.at[sweep, index],
            device_id={"dom": dom + neighbour_offsets[index]},
        )

    sub = lax.broadcasted_iota(jnp.int32, (ROWS, LANES), 0)
    block_lane = sub * cap + lane % cap

    def pack(values):
        packed = jnp.zeros((ROWS, LANES), F32)
        for row in range(NLOAD):
            packed = jnp.where(lane_block == row, lane_gather(spread(values[row : row + 1]), block_lane), packed)
        return packed

    def unpack(rows):
        values = jnp.zeros((ROWS, LANES), F32)
        for part, row in enumerate(rows):
            values = jnp.where(lane_block == part, lane_gather(spread(row), block_lane), values)
        return values

    def two_terms(values):
        first = values.astype(BF16)
        second = (values - first.astype(F32)).astype(BF16)
        return jnp.concatenate([first, second], axis=0)

    def picked(lhs, hot, high, first_high, value):
        found = lax.dot_general(lhs, hot, (((1,), (0,)), ((), ())), preferred_element_type=F32)
        for at in range(lhs.shape[0] // (2 * ROWS)):
            base = 2 * ROWS * at
            part = found[base : base + ROWS] + found[base + ROWS : base + 2 * ROWS]
            value = jnp.where(high == first_high + at, part, value)
        return value

    def set_state_lhs():
        for at in range(cells // WIDE):
            state_lhs[2 * ROWS * at : 2 * ROWS * (at + 1)] = two_terms(state_buf[:, at * WIDE : (at + 1) * WIDE])

    def live_mask(tile):
        limit = jnp.zeros((ROWS, LANES), jnp.int32)
        for part in range(per_tile):
            limit = jnp.where(lane_block == part, surf_count[0, 0, tile * per_tile + part], limit)
        return (lane % cap) < limit

    def state_tiles():
        return [state_buf[:, at * LANES : (at + 1) * LANES] for at in range(tiles)]

    def prepare(sweep):
        for at in range(ghosts // WIDE):
            columns = slice(at * WIDE, (at + 1) * WIDE)
            high = spread(list_v[0, :, columns]) // WIDE
            start = jnp.zeros((ROWS, WIDE), F32)
            out_buf[sweep, :, columns] = picked(state_lhs[...], out_hot[:, columns], high, 0, start)

    def map_rows(row, tile):
        if surf_tiles == 1:
            return map_v[row * NVAR : (row + 1) * NVAR, :]
        return map_v[pl.ds(row * NVAR * surf_tiles + tile, NVAR, stride=surf_tiles), :]

    def prepare_surface(sweep):
        own = state_tiles()

        @pl.when(is_structure)
        def _():
            for section in range(flow):
                for tile in range(surf_tiles):
                    index = spread(node_v[section, :, tile * LANES : (tile + 1) * LANES])
                    packed = pack(gather_tiles(own, index // LANES, index % LANES))
                    for part in range(per_tile):
                        disp_send[sweep, section * n_dom + tile * per_tile + part] = packed[part : part + 1]

        @pl.when(jnp.logical_not(is_structure))
        def _():
            for tile in range(surf_tiles):
                columns = slice(tile * LANES, (tile + 1) * LANES)
                index = spread(cell_v[0, :, columns])
                values = gather_tiles(own, index // LANES, index % LANES)
                loads = sum_rows([pad_rows(map_rows(row, tile) * values[:NVAR]) for row in range(NLOAD)])
                packed = pack(jnp.where(live_mask(tile), loads, 0.0))
                for part in range(per_tile):
                    load_send[sweep, tile * per_tile + part] = packed[part : part + 1]

    def send_halo(sweep):
        for index in range(NBR):

            @pl.when(present(neighbour_offsets[index]))
            def _():
                halo_copy(sweep, index).start()

    def send_surface(sweep):
        @pl.when(is_structure)
        def _():
            @pl.loop(0, flow * n_dom)
            def _(at):
                section, part = at // n_dom, at % n_dom
                pltpu.make_async_remote_copy(
                    src_ref=disp_send.at[sweep, at],
                    dst_ref=disp_recv.at[sweep, dom],
                    send_sem=surf_send_sem.at[sweep],
                    recv_sem=disp_recv_sem.at[sweep],
                    device_id={"sec": section, "dom": part},
                ).start()

        @pl.when(jnp.logical_not(is_structure))
        def _():
            @pl.loop(0, n_dom)
            def _(at):
                pltpu.make_async_remote_copy(
                    src_ref=load_send.at[sweep, at],
                    dst_ref=load_recv.at[sweep, sec * n_dom + dom],
                    send_sem=surf_send_sem.at[sweep],
                    recv_sem=load_recv_sem.at[sweep],
                    device_id={"sec": flow, "dom": at},
                ).start()

    def one_hot(low, rows):
        row = lax.broadcasted_iota(jnp.int32, (rows, low.shape[1]), 0)
        return jnp.where(row == low, 1.0, 0.0).astype(BF16)

    def build_list_hot():
        for at in range(ghosts // WIDE):
            columns = slice(at * WIDE, (at + 1) * WIDE)
            out_hot[:, columns] = one_hot(list_v[0, :, columns] % WIDE, WIDE)

    def build_source_hot():
        @pl.loop(0, faces // CHUNK)
        def _(at):
            columns = pl.ds(pl.multiple_of(at * CHUNK, CHUNK), CHUNK)
            source_hot[:, columns] = one_hot(source_v[0, :, columns] % WIDE, WIDE)

    def build_target_hot():
        @pl.loop(0, faces // CHUNK)
        def _(at):
            columns = pl.ds(pl.multiple_of(at * CHUNK, CHUNK), CHUNK)
            onehot[:, columns] = one_hot(target_v[0, :, columns] % LOW, LOW)

    def local_gather():
        @pl.loop(0, faces // CHUNK)
        def _(at):
            columns = pl.ds(pl.multiple_of(at * CHUNK, CHUNK), CHUNK)
            high = spread(source_v[0, :, columns]) // WIDE
            start = jnp.zeros((ROWS, CHUNK), F32)
            gath[:, columns] = picked(state_lhs[...], source_hot[:, columns], high, 0, start)

    def receive_halo(sweep):
        for index in range(NBR):

            @pl.when(present(-neighbour_offsets[index]))
            def _():
                halo_copy(sweep, index).wait_recv()

        for at in range(ghost_tiles):
            total = jnp.zeros((ROWS, LANES), F32)
            for index in range(NBR):
                start, end, first, last = piece_tiles(index)
                if first <= at < last:
                    inside = (lane + at * LANES >= start) & (lane + at * LANES < end)
                    part = halo_recv[sweep, index, :, (at - first) * LANES : (at - first + 1) * LANES]
                    total = jnp.where(inside, part, total)
            ghost_buf[:, at * LANES : (at + 1) * LANES] = total
        for at in range(ghosts // WIDE):
            ghost_lhs[2 * ROWS * at : 2 * ROWS * (at + 1)] = two_terms(ghost_buf[:, at * WIDE : (at + 1) * WIDE])

    def masked_dot(values, high, rhs):
        both = two_terms(values)
        high = jnp.broadcast_to(high.astype(F32), both.shape).astype(BF16)
        lhs = jnp.concatenate(
            [jnp.where(high == at, both, jnp.zeros_like(both)) for at in range(highs)], axis=0
        )
        return lax.dot_general(lhs, rhs, (((1,), (1,)), ((), ())), preferred_element_type=F32)

    def face_pass():
        def step(at, total):
            base = at * CHUNK
            columns = pl.ds(pl.multiple_of(base, CHUNK), CHUNK)
            high = spread(source_v[0, :, columns]) // WIDE
            value = picked(ghost_lhs[...], source_hot[:, columns], high, cells // WIDE, gath[:, columns])
            pieces = []
            for piece in range(CHUNK // LANES):
                part = pl.ds(pl.multiple_of(base + piece * LANES, LANES), LANES)
                here = value[:NVAR, piece * LANES : (piece + 1) * LANES]
                pieces.append(
                    sum_rows([pad_rows(block_v[0, 0, row, :, part].astype(F32) * here) for row in range(NVAR)])
                )
            contrib = jnp.concatenate(pieces, axis=1)
            entry = lax.broadcasted_iota(jnp.int32, (1, CHUNK), 1) + base
            high = jnp.where(entry < live_faces, target_v[0, :, columns] // LOW, highs)
            return total + masked_dot(contrib, high, onehot[:, columns])

        return lax.fori_loop(0, faces // CHUNK, step, jnp.zeros((2 * ROWS * highs, LOW), F32))

    def surface_pass(sweep):
        @pl.when(is_structure)
        def _():
            pltpu.make_async_copy(load_recv.at[sweep], load_recv.at[sweep], load_recv_sem.at[sweep]).wait()

        @pl.when(jnp.logical_not(is_structure))
        def _():
            pltpu.make_async_copy(disp_recv.at[sweep], disp_recv.at[sweep], disp_recv_sem.at[sweep]).wait()

        total = None
        for section in range(flow):
            for tile in range(surf_tiles):
                columns = slice(tile * LANES, (tile + 1) * LANES)
                first = section * n_dom + tile * per_tile
                values = unpack([load_recv[sweep, first + part] for part in range(per_tile)])
                cell = node_v[section, :, columns]
                if section == 0:
                    back = unpack([disp_recv[sweep, tile * per_tile + part] for part in range(per_tile)])
                    back = jnp.where(live_mask(tile), back, 0.0)
                    pushed = map_rows(0, tile) * back[0:1]
                    for row in range(1, NLOAD):
                        pushed = pushed + map_rows(row, tile) * back[row : row + 1]
                    values = jnp.where(is_structure, values, pad_rows(pushed))
                    cell = jnp.where(is_structure, cell, cell_v[0, :, columns])
                else:
                    values = jnp.where(is_structure, values, 0.0)
                term = masked_dot(values, cell // LOW, one_hot(cell % LOW, LOW))
                total = term if total is None else total + term
        return total

    fetches[0].wait()
    for at in range(tiles):
        state_buf[:, at * LANES : (at + 1) * LANES] = pad_rows(init_v[pl.ds(at, NVAR, stride=tiles), :])
    set_state_lhs()
    fetches[1].wait()
    build_list_hot()
    prepare(0)
    pl.semaphore_wait(barrier, n_dom - 1 + partners)
    greet(ready_sem)
    send_halo(0)
    for fetch in fetches[2:6]:
        fetch.wait()
    prepare_surface(0)
    build_source_hot()
    pl.semaphore_wait(ready_sem, partners)
    send_surface(0)
    fetches[6].wait()
    build_target_hot()
    for fetch in fetches[7:]:
        fetch.wait()
    for sweep in range(ITERS):
        if sweep > 0:
            prepare(sweep)
            send_halo(sweep)
            prepare_surface(sweep)
            send_surface(sweep)
        local_gather()
        receive_halo(sweep)
        total = face_pass()
        total = total + surface_pass(sweep)
        for at in range(tiles):
            base = 2 * ROWS * (at * LANES // LOW)
            columns = slice(at * LANES % LOW, at * LANES % LOW + LANES)
            gone = total[base : base + ROWS, columns] + total[base + ROWS : base + 2 * ROWS, columns]
            rest = right_v[pl.ds(at, NVAR, stride=tiles), :] - gone[:NVAR]
            fresh = sum_rows(
                [
                    pad_rows(inverse_v[pl.ds(row * NVAR * tiles + at, NVAR, stride=tiles), :] * rest)
                    for row in range(NVAR)
                ]
            )
            if sweep == ITERS - 1:
                out_ref[pl.ds(at, NVAR, stride=tiles), :] = fresh[:NVAR]
            else:
                state_buf[:, at * LANES : (at + 1) * LANES] = fresh
        if sweep < ITERS - 1:
            set_state_lhs()

    for sweep in range(ITERS):
        for index in range(NBR):

            @pl.when(present(neighbour_offsets[index]))
            def _():
                halo_copy(sweep, index).wait_send()

        @pl.when(is_structure)
        def _():
            pltpu.make_async_copy(load_recv.at[sweep], load_recv.at[sweep], surf_send_sem.at[sweep]).wait()

        @pl.when(jnp.logical_not(is_structure))
        def _():
            pltpu.make_async_copy(disp_recv.at[sweep], disp_recv.at[sweep], surf_send_sem.at[sweep]).wait()


def body(n_sec, n_dom, *args):
    cells = args[0].shape[-1]
    faces = args[4].shape[-1]
    ghosts = args[7].shape[-1]
    slots = args[8].shape[-1]
    flow = n_sec - 1
    piece = (2 * LANES - 1 + ghosts // NBR) // LANES * LANES
    vmem = pl.BlockSpec(memory_space=pltpu.VMEM)
    smem = pl.BlockSpec(memory_space=pltpu.SMEM)
    specs = [pl.BlockSpec(memory_space=pltpu.HBM)] * 12
    specs[6] = smem
    specs[9] = smem
    args = list(args)
    for at in (0, 1, 2, 10):
        args[at] = args[at].reshape(-1, LANES)
    fetched = [args[at] for at in (0, 1, 2, 3, 4, 5, 7, 8, 10, 11)]
    wide_rows = 2 * ROWS * (cells // WIDE)
    ghost_rows = 2 * ROWS * (ghosts // WIDE)
    out = pl.pallas_call(
        functools.partial(kernel, (n_sec, n_dom, cells, faces, slots, ghosts)),
        out_shape=jax.ShapeDtypeStruct(args[0].shape, F32),
        in_specs=specs,
        out_specs=vmem,
        scratch_shapes=[
            *[pltpu.VMEM(value.shape, value.dtype) for value in fetched],
            pltpu.VMEM((ROWS, cells), F32),
            pltpu.VMEM((wide_rows, WIDE), BF16),
            pltpu.VMEM((ghost_rows, WIDE), BF16),
            pltpu.VMEM((WIDE, ghosts), BF16),
            pltpu.VMEM((WIDE, faces), BF16),
            pltpu.VMEM((ITERS, ROWS, ghosts), F32),
            pltpu.VMEM((ITERS, NBR, ROWS, piece), F32),
            pltpu.VMEM((ROWS, ghosts), F32),
            pltpu.VMEM((ROWS, faces), F32),
            pltpu.VMEM((LOW, faces), BF16),
            pltpu.VMEM((ITERS, n_dom, 1, LANES), F32),
            pltpu.VMEM((ITERS, flow * n_dom, 1, LANES), F32),
            pltpu.VMEM((ITERS, flow * n_dom, 1, LANES), F32),
            pltpu.VMEM((ITERS, n_dom, 1, LANES), F32),
            pltpu.SemaphoreType.DMA((ITERS, NBR)),
            pltpu.SemaphoreType.DMA((ITERS, NBR)),
            pltpu.SemaphoreType.DMA((ITERS,)),
            pltpu.SemaphoreType.DMA((ITERS,)),
            pltpu.SemaphoreType.DMA((ITERS,)),
            pltpu.SemaphoreType.DMA((len(fetched),)),
            pltpu.SemaphoreType.REGULAR,
        ],
        compiler_params=pltpu.CompilerParams(
            collective_id=0, has_side_effects=True, vmem_limit_bytes=63 * 1024 * 1024 + 768 * 1024
        ),
    )(*args)
    return out.reshape(1, 1, NVAR, cells)


def solution(mesh):
    in_specs = (
        P("sec", "dom", None, None),
        P("sec", "dom", None, None),
        P("sec", "dom", None, None, None),
        P("sec", "dom", None, None, None),
        P("sec", "dom", None),
        P("sec", "dom", None),
        P("sec", "dom"),
        P("sec", "dom", None),
        P("sec", "dom", None),
        P("sec", "dom", None),
        P("sec", "dom", None, None, None),
        P(None, "dom", None),
    )
    out_specs = P("sec", "dom", None, None)
    run = functools.partial(body, mesh.shape["sec"], mesh.shape["dom"])
    return jax.shard_map(run, mesh=mesh, in_specs=in_specs, out_specs=out_specs, check_vma=False)
```

time: 35.2 us -> 24.4 us (0.69)
  Pallas kernels: 29.8 us -> 20.8 us
  local copies, waits for them, and re-layouts: 4.36 us -> 1.99 us
  other arithmetic: 0 us -> 0.73 us
    pallas_call x1, Pallas kernels: 29.8 us -> 20.8 us  [body(): pl.pallas_call(functools.partial(kernel, (n_sec, n_dom, cells, faces, slo...]
    unnamed x20 -> x1, local copies, waits for them, and re-layouts: 3.7 us -> 1.39 us
    unnamed x0 -> x1, other arithmetic: none -> 0.73 us
    pallas_call x1 -> x0, local copies, waits for them, and re-layouts: 0.66 us -> none  [body(): pl.pallas_call(functools.partial(kernel, (n_sec, n_dom, cells, faces, slo...]
    reshape x0 -> x1, local copies, waits for them, and re-layouts: none -> 0.6 us  [body(): args[at] = args[at].reshape(-1, LANES)]
where the time goes in v2:
time: 24.4 us; the launch traced here: 24.1 us
  Pallas kernels  20.8 us (85%)
  local copies, waits for them, and re-layouts  1.99 us (8%)
  other arithmetic  0.73 us (3%)
  between operations  0.66 us (3%)
    pallas_call x1, Pallas kernels, body(): pl.pallas_call(functools.partial(kernel, (n_sec, n_dom, cells, faces, slo...  20.8 us
    unnamed x1, local copies, waits for them, and re-layouts  1.39 us
    unnamed x1, other arithmetic  0.73 us
    reshape x1, local copies, waits for them, and re-layouts, body(): args[at] = args[at].reshape(-1, LANES)  0.6 us

profile of v2, /device:TPU:0, one launch (start us, length us, event | category | flops | bytes accessed | tf_op | source)
XLA Modules:
  0.0 24.1 jit_solution(6317659592142762700)
XLA Ops:
  0.7 0.7 %reduce = f32[3,6,128]{2,1,0:T(8,128)S(1)} reduce(f32[1,1,3,6,128]{4,1,3,2,0:T(1,128)} %param.22, f32[]{:T(128)} %constant.12), dimensions={0,1}, to_apply=%param.22.reduce_sub_computation | reduce | bytes 18436 | tf_op args[10]
  1.4 0.6 %reshape.18.surf_map = f32[18,128]{1,0:T(8,128)} reshape(f32[3,6,128]{2,1,0:T(8,128)S(1)} %reduce) | data formatting | bytes 18432 | tf_op jit(solution)/shard_map/reshape | solution.py:489
  2.0 20.8 %shard_map.118 = f32[72,128]{1,0:T(8,128)} custom-call(f32[72,128]{1,0:T(8,128)} %bitcast.6, f32[72,128]{1,0:T(8,128)} %bitcast.7, f32[432,128]{1,0:T(8,128)} %bitcast.4, bf16[1,1,6,6,9216]{4,3,2,1,0:T(8,128)(2,1)} %face_block.1, s32[1,1,9216]{2,1,0:T(1,128)} %face_target.1, s32[1,1,9216]{2,1,0:T(1,128)} %face_source.1, s32[1,1]{1,0:T(1,128)S(6)} %copy.17.face_count, ...), custom_call_target="tpu_custom_call" | custom-call | tf_op jit(solution)/shard_map/pallas_call | solution.py:493
  22.8 1.4 %copy.18 = f32[1,1,6,1536]{3,1,2,0:T(1,128)} copy(f32[1,1,6,1536]{3,1,2,0:T(1,128)} %bitcast.5) | data formatting | bytes 73728
